TPU v7x, 512 devices: a whole 4x8x8 slice. The times are simulated.
512 devices in a mesh: len: 64 (over x, z, core), wid: 8 (over y).
Axes of the slice: x: 4, y: 8, z: 8, core: 2. Of those that a mesh axis runs over, the one named last changes fastest.
Arguments:
- flow_state: float32 [3, 512, 16, 2048], P(None, 'len', None, 'wid'), may hold values from -0.5 to 2
- courant: float32 [512, 16, 2048], P('len', None, 'wid'), as said below
- inflow: float32 [3, 16, 2048], P(None, None, 'wid'), may hold values from -6 to 6
- height_ops: float32 [8, 16, 16], replicated, may hold values from -1.5 to 1.5
- metric_index: int32 [128], P('len'), may hold values from 0 to 7
Outputs:
- new_state: float32 [3, 512, 16, 2048], P(None, 'len', None, 'wid')
- tendency: float32 [3, 512, 16, 2048], P(None, 'len', None, 'wid')
Inputs may be any that keep to these rules, and one draw needn't show every extreme that they name: courant is positive.
All inputs are finite; a program needn't handle non-finite values.
Results may differ from a plain program's by a relative error of at most 0.0003.
Values sent between devices are 32-bit elements; how exact they have to be, the bound alone decides.
A program may use at most 64 MiB of HBM per device.

v0:
```python
import functools

import jax
import jax.numpy as jnp
from jax import lax
from jax.experimental import pallas as pl
from jax.experimental.pallas import tpu as pltpu
from jax.sharding import PartitionSpec as P

STEP = 0.25
LANE = 128
SUB = 8
MESH = pl.DeviceIdType.MESH


def split_bf16(value):
    high = value.astype(jnp.bfloat16)
    return high, (value - high.astype(jnp.float32)).astype(jnp.bfloat16)


def sweep_kernel(
    inner, outer, nwid, groups,
    flow_hbm, cour_hbm, inflow_hbm, ops_hbm, metric_hbm,
    new_ref, tend_ref,
    flow, cour, infl, ops, metric, prod, halo_out, halo_in,
    send1, recv1, send2, recv2, send3, recv3,
    in_sem, halo_send, halo_recv, ex_send, ex_recv,
):
    fields, nx, nz, ny = flow.shape
    nh, nl = nz // SUB, ny // LANE
    per = nz // inner
    chunk = per * SUB
    me = lax.axis_index("len")
    wid = lax.axis_index("wid")
    mine = lax.rem(me, inner)
    block = lax.div(me, inner)
    right, left = lax.rem(wid + 1, nwid), lax.rem(wid + nwid - 1, nwid)

    loads = [
        pltpu.make_async_copy(src, dst, in_sem.at[i])
        for i, (src, dst) in enumerate(
            ((flow_hbm, flow), (cour_hbm, cour), (inflow_hbm, infl), (ops_hbm, ops), (metric_hbm, metric))
        )
    ]
    for load in loads:
        load.start()

    def group_peer(j):
        return lax.rem(mine + j, inner)

    def block_peer(j):
        return lax.rem(block + j, outer)

    barrier = pltpu.get_barrier_semaphore()
    pl.semaphore_signal(barrier, inc=1, device_id=(me, left), device_id_type=MESH)
    pl.semaphore_signal(barrier, inc=1, device_id=(me, right), device_id_type=MESH)
    for j in range(1, inner):
        pl.semaphore_signal(
            barrier, inc=1, device_id=(block * inner + group_peer(j), wid), device_id_type=MESH
        )
    for j in range(1, outer):
        pl.semaphore_signal(
            barrier, inc=1, device_id=(block_peer(j) * inner + mine, wid), device_id_type=MESH
        )

    loads[4].wait()
    loads[3].wait()
    rows = nx * nz
    tiles = []
    for g in range(groups):
        one = ops[metric[g]]
        tiles.append(jnp.concatenate([one] * nx, axis=1))
    row_cell = lax.broadcasted_iota(jnp.int32, (nz, rows), 1) // nz
    diag = jnp.concatenate(
        [jnp.where(row_cell == i, tiles[i * groups // nx], 0.0) for i in range(nx)], axis=0
    )
    diag_high, diag_low = split_bf16(diag)

    loads[1].wait()
    take = []
    keep = []
    for i in range(nx):
        c = cour[i]
        t = 1.0 / (1.0 + c)
        take.append(t)
        keep.append(jnp.where(c < 1.0, c * t, 1.0 - t))
        prod[i] = keep[i] if i == 0 else keep[i] * prod[i - 1]

    loads[2].wait()
    row = lax.broadcasted_iota(jnp.int32, (SUB, LANE), 0)
    lane = lax.broadcasted_iota(jnp.int32, (SUB, LANE), 1)
    slot, spot = lane // 4, lane % 4
    height = lax.broadcasted_iota(jnp.int32, (nz, LANE), 0)
    starts = []
    for p in range(per):
        tile = jnp.zeros((SUB, LANE), jnp.float32)
        for f in range(fields):
            for l in range(nl):
                line = jnp.where(height == mine * per + p, infl[f, :, l * LANE:(l + 1) * LANE], 0.0)
                line = jnp.sum(line, axis=0, keepdims=True)
                tile = jnp.where(row == (1 + f) * nl + l, jnp.broadcast_to(line, (SUB, LANE)), tile)
        starts.append(tile)

    loads[0].wait()
    nrow = fields * nx * nh
    slots = LANE // 4
    npack = pl.cdiv(nrow, slots)

    def where_is(r):
        f, i, h = r // (nx * nh), (r // nh) % nx, r % nh
        return f, i, slice(h * SUB, (h + 1) * SUB)

    packed = []
    for v in range(npack):
        low = jnp.zeros((SUB, LANE), jnp.float32)
        high = low
        for s in range(min(slots, nrow - v * slots)):
            f, i, z = where_is(v * slots + s)
            here = slot == s
            first, last = flow[f, i, z, :LANE], flow[f, i, z, ny - LANE:]
            low = jnp.where(here, pltpu.roll(first, 4 * s, 1) if s else first, low)
            high = jnp.where(here, pltpu.roll(last, (4 * s + 3) % LANE, 1), high)
        low = jnp.where(spot < 3, low, 0.0)
        high = jnp.where(spot < 3, high, 0.0)
        packed.append((low, high))
        halo_out[0, v] = low
        halo_out[1, v] = high

    pl.semaphore_wait(barrier, 2 + (inner - 1) + (outer - 1))
    halos = [
        pltpu.make_async_remote_copy(
            src_ref=halo_out.at[side],
            dst_ref=halo_in.at[side],
            send_sem=halo_send.at[side],
            recv_sem=halo_recv.at[side],
            device_id=(me, to),
            device_id_type=MESH,
        )
        for side, to in ((0, left), (1, right))
    ]
    for halo in halos:
        halo.start()

    for f in range(fields):
        q = flow[f].reshape(rows, ny)
        q_high, q_low = split_bf16(q)
        vertical = jnp.dot(diag_high, q_high, preferred_element_type=jnp.float32)
        vertical += jnp.dot(diag_low, q_high, preferred_element_type=jnp.float32)
        vertical += jnp.dot(diag_high, q_low, preferred_element_type=jnp.float32)
        for i in range(nx):
            q = flow[f, i]
            slopes = jnp.zeros((nz, ny), jnp.float32)
            for offset, factor in ((1, 45.0 / 60.0), (2, -9.0 / 60.0), (3, 1.0 / 60.0)):
                slopes += factor * (pltpu.roll(q, ny - offset, 1) - pltpu.roll(q, offset, 1))
            tend_ref[f, i] = vertical[i * nz:(i + 1) * nz] - flow[1, i] * slopes

    for halo in halos:
        halo.wait_recv()
    for v in range(npack):
        low, high = packed[v]
        before = jnp.where(wid == 0, 0.0, halo_in[1, v]) - high
        after = jnp.where(wid == nwid - 1, 0.0, halo_in[0, v]) - low
        fix_low = (
            (-1.0 / 60.0) * before
            + jnp.where(spot < 2, 9.0 / 60.0, 0.0) * pltpu.roll(before, LANE - 1, 1)
            + jnp.where(spot < 1, -45.0 / 60.0, 0.0) * pltpu.roll(before, LANE - 2, 1)
        )
        fix_high = (
            (1.0 / 60.0) * after
            + jnp.where(spot >= 1, -9.0 / 60.0, 0.0) * pltpu.roll(after, 1, 1)
            + jnp.where(spot >= 2, 45.0 / 60.0, 0.0) * pltpu.roll(after, 2, 1)
        )
        for s in range(min(slots, nrow - v * slots)):
            f, i, z = where_is(v * slots + s)
            fix = pltpu.roll(fix_low, LANE - 4 * s, 1) if s else fix_low
            fix = jnp.where(lane < 3, fix, 0.0)
            tend_ref[f, i, z, :LANE] -= flow[1, i, z, :LANE] * fix
            fix = pltpu.roll(fix_high, (2 * LANE - 3 - 4 * s) % LANE, 1)
            fix = jnp.where(lane >= LANE - 3, fix, 0.0)
            tend_ref[f, i, z, ny - LANE:] -= flow[1, i, z, ny - LANE:] * fix

    for f in range(fields):
        state = None
        for i in range(nx):
            c = cour[i]
            t = 1.0 / (1.0 + c)
            k = jnp.where(c < 1.0, c * t, 1.0 - t)
            gain = t * (flow[f, i] + STEP * tend_ref[f, i])
            state = gain if state is None else k * state + gain
            new_ref[f, i] = state

    def scatter(value, v):
        for h in range(nh):
            for l in range(nl):
                send1[pl.ds(h * SUB * SUB + v * nl + l, SUB, stride=SUB), :] = value[
                    h * SUB:(h + 1) * SUB, l * LANE:(l + 1) * LANE
                ]

    scatter(prod[nx - 1], 0)
    for f in range(fields):
        scatter(new_ref[f, nx - 1], 1 + f)

    def part(ref, k):
        return ref.at[pl.ds(pl.multiple_of(k * chunk, SUB), chunk), :]

    def exchange(source_of, into, at, peers, phase):
        for peer, device in peers:
            pltpu.make_async_remote_copy(
                src_ref=source_of(peer),
                dst_ref=part(into, at),
                send_sem=ex_send.at[phase],
                recv_sem=ex_recv.at[phase],
                device_id=(device, wid),
                device_id_type=MESH,
            ).start()

    def total(ref, count, phase):
        span = ref.at[pl.ds(0, count * chunk), :]
        return pltpu.make_async_remote_copy(
            src_ref=span,
            dst_ref=span,
            send_sem=ex_send.at[phase],
            recv_sem=ex_recv.at[phase],
            device_id=(me, right),
            device_id_type=MESH,
        )

    group = [(group_peer(j), block * inner + group_peer(j)) for j in range(1, inner)]
    blocks = [(block_peer(j), block_peer(j) * inner + mine) for j in range(1, outer)]

    exchange(lambda k: part(send1, k), recv1, mine, group, 0)
    own = pl.ds(pl.multiple_of(mine * chunk, SUB), chunk)
    recv1[own, :] = send1[own, :]
    total(recv1, inner - 1, 0).wait_recv()

    def load_map(ref, at):
        tile = ref[at:at + SUB, :]
        decay = jnp.broadcast_to(tile[0:1], (SUB, LANE))
        for l in range(1, nl):
            decay = jnp.where(row % nl == l, jnp.broadcast_to(tile[l:l + 1], (SUB, LANE)), decay)
        return decay, tile

    prefix = []
    for p in range(per):
        decay, state = jnp.ones((SUB, LANE), jnp.float32), jnp.zeros((SUB, LANE), jnp.float32)
        line = []
        for k in range(inner):
            line.append((decay, state))
            d, s = load_map(recv1, k * chunk + p * SUB)
            decay, state = d * decay, d * state + s
        prefix.append(line)
        send2[p * SUB:(p + 1) * SUB, :] = jnp.where(row < nl, decay, state)

    if outer > 1:
        exchange(lambda k: send2, recv2, block, blocks, 1)
        own = pl.ds(pl.multiple_of(block * chunk, SUB), chunk)
        recv2[own, :] = send2[...]
        total(recv2, outer - 1, 1).wait_recv()
    for p in range(per):
        entry = starts[p]
        for b in range(outer - 1):
            d, s = load_map(recv2, b * chunk + p * SUB)
            entry = jnp.where(b < block, d * entry + s, entry)
        for k in range(inner):
            d, s = prefix[p][k]
            send3[k * chunk + p * SUB:k * chunk + (p + 1) * SUB, :] = d * entry + s

    exchange(lambda k: part(send3, k), recv3, mine, group, 2)
    own = pl.ds(pl.multiple_of(mine * chunk, SUB), chunk)
    recv3[own, :] = send3[own, :]
    total(recv3, inner - 1, 2).wait_recv()
    for f in range(fields):
        for h in range(nh):
            for l in range(nl):
                enter = recv3[pl.ds(h * SUB * SUB + (1 + f) * nl + l, SUB, stride=SUB), :]
                z, y = slice(h * SUB, (h + 1) * SUB), slice(l * LANE, (l + 1) * LANE)
                for i in range(nx):
                    new_ref[f, i, z, y] += prod[i, z, y] * enter

    for halo in halos:
        halo.wait_send()
    total(send1, inner - 1, 0).wait_send()
    if outer > 1:
        total(recv2, outer - 1, 1).wait_send()
    total(send3, inner - 1, 2).wait_send()


def shards(inner, flow_state, courant, inflow, height_ops, metric_index):
    fields, nx, nz, ny = flow_state.shape
    count = lax.axis_size("len")
    nwid = lax.axis_size("wid")
    outer = count // inner
    chunk = nz // inner * SUB
    out = jax.ShapeDtypeStruct(flow_state.shape, jnp.float32)
    anywhere = pl.BlockSpec(memory_space=pl.ANY)
    nrow = fields * nx * (nz // SUB)
    npack = pl.cdiv(nrow, LANE // 4)
    f32 = jnp.float32
    dma = pltpu.SemaphoreType.DMA
    return pl.pallas_call(
        functools.partial(sweep_kernel, inner, outer, nwid, metric_index.shape[0]),
        out_shape=(out, out),
        in_specs=[anywhere] * 5,
        out_specs=(pl.BlockSpec(memory_space=pltpu.VMEM),) * 2,
        scratch_shapes=[
            pltpu.VMEM(flow_state.shape, f32),
            pltpu.VMEM(courant.shape, f32),
            pltpu.VMEM(inflow.shape, f32),
            pltpu.VMEM(height_ops.shape, f32),
            pltpu.SMEM(metric_index.shape, jnp.int32),
            pltpu.VMEM(courant.shape, f32),
            pltpu.VMEM((2, npack, SUB, LANE), f32),
            pltpu.VMEM((2, npack, SUB, LANE), f32),
            pltpu.VMEM((inner * chunk, LANE), f32),
            pltpu.VMEM((inner * chunk, LANE), f32),
            pltpu.VMEM((chunk, LANE), f32),
            pltpu.VMEM((outer * chunk, LANE), f32),
            pltpu.VMEM((inner * chunk, LANE), f32),
            pltpu.VMEM((inner * chunk, LANE), f32),
            dma((5,)),
            dma((2,)),
            dma((2,)),
            dma((3,)),
            dma((3,)),
        ],
        compiler_params=pltpu.CompilerParams(collective_id=0, has_side_effects=True),
        name="sweep",
    )(flow_state, courant, inflow, height_ops, metric_index)


def solution(mesh, inner=16):
    placed = (
        P(None, "len", None, "wid"),
        P("len", None, "wid"),
        P(None, None, "wid"),
        P(),
        P("len"),
    )
    return jax.shard_map(
        functools.partial(shards, inner),
        mesh=mesh,
        in_specs=placed,
        out_specs=(P(None, "len", None, "wid"), P(None, "len", None, "wid")),
        check_vma=False,
    )
```

profile of v0, /device:TPU:1, one launch (start us, length us, event | category | flops | bytes accessed | tf_op | source)
XLA Modules:
  0.0 35.4 jit_solution(3893454809997487215)
XLA Ops:
  0.6 32.2 %sweep.1 = (f32[3,8,16,256]{3,2,1,0:T(8,128)}, f32[3,8,16,256]{3,2,1,0:T(8,128)}) custom-call(f32[3,8,16,256]{3,2,1,0:T(8,128)} %flow_hbm.1, f32[8,16,256]{2,1,0:T(8,128)} %cour_hbm.1, f32[3,16,256]{2,1,0:T(8,128)} %inflow_hbm.1, f32[8,16,16]{2,1,0:T(8,128)} %ops_hbm.1, s32[2]{0:T(128)} %metric_hbm.1), custom_call_target="tpu_custom_call" | custom-call | tf_op jit(solution)/shard_map/sweep/pallas_call | solution.py:300
  32.9 0.0 copy-start
  32.9 1.8 %copy.9 = f32[3,8,16,256]{3,2,1,0:T(8,128)} copy(f32[3,8,16,256]{3,2,1,0:T(8,128)} %get-tuple-element.4) | data formatting | bytes 786432
  34.7 0.0 copy-done
  34.7 0.7 %copy.10 = f32[3,8,16,256]{3,2,1,0:T(8,128)} copy(f32[3,8,16,256]{3,2,1,0:T(8,128)S(1)} %copy-done) | data formatting | bytes 786432
Async XLA Ops:
  32.9 1.8 %copy-start = (f32[3,8,16,256]{3,2,1,0:T(8,128)S(1)}, f32[3,8,16,256]{3,2,1,0:T(8,128)}, u32[]{:S(2)}) copy-start(f32[3,8,16,256]{3,2,1,0:T(8,128)} %get-tuple-element.5) | copy-start | bytes 1179652
where the time goes:
time: 35.6 us; the launch traced here: 35.4 us
  Pallas kernels  32.2 us (90%)
  local copies, waits for them, and re-layouts  2.57 us (7%)
  between operations  0.65 us (2%)
    pallas_call x1, Pallas kernels, shards(): pl.pallas_call(functools.partial(sweep_kernel, inner, outer, nwid, metric...  32.2 us
    unnamed x4, local copies, waits for them, and re-layouts  2.57 us

commit v1 on v0

--- a/solution.py
+++ b/solution.py
@@ -28,7 +28,9 @@
 ):
     fields, nx, nz, ny = flow.shape
     nh, nl = nz // SUB, ny // LANE
-    per = nz // inner
+    owners = inner // 2
+    shift = inner * 3 // 4
+    per = nz // owners
     chunk = per * SUB
     me = lax.axis_index("len")
     wid = lax.axis_index("wid")
@@ -45,23 +47,30 @@
     for load in loads:
         load.start()
 
-    def group_peer(j):
-        return lax.rem(mine + j, inner)
-
-    def block_peer(j):
-        return lax.rem(block + j, outer)
+    rank = lax.rem(mine + (inner - shift), inner)
+    owner = rank < owners
+    owner_order = list(range(owners // 2, owners))[::-1] + list(range(owners // 2))
 
     barrier = pltpu.get_barrier_semaphore()
-    pl.semaphore_signal(barrier, inc=1, device_id=(me, left), device_id_type=MESH)
-    pl.semaphore_signal(barrier, inc=1, device_id=(me, right), device_id_type=MESH)
-    for j in range(1, inner):
-        pl.semaphore_signal(
-            barrier, inc=1, device_id=(block * inner + group_peer(j), wid), device_id_type=MESH
-        )
-    for j in range(1, outer):
-        pl.semaphore_signal(
-            barrier, inc=1, device_id=(block_peer(j) * inner + mine, wid), device_id_type=MESH
-        )
+
+    def greet(to, across):
+        pl.semaphore_signal(barrier, inc=1, device_id=(to, across), device_id_type=MESH)
+
+    greet(me, left)
+    greet(me, right)
+    for k in range(inner):
+        met = mine != k
+        if (k - shift) % inner >= owners:
+            met = jnp.logical_and(met, owner)
+
+        @pl.when(met)
+        def _():
+            greet(block * inner + k, wid)
+
+    @pl.when(owner)
+    def _():
+        for j in range(1, outer):
+            greet(lax.rem(block + j, outer) * inner + mine, wid)
 
     loads[4].wait()
     loads[3].wait()
@@ -96,7 +105,7 @@
         tile = jnp.zeros((SUB, LANE), jnp.float32)
         for f in range(fields):
             for l in range(nl):
-                line = jnp.where(height == mine * per + p, infl[f, :, l * LANE:(l + 1) * LANE], 0.0)
+                line = jnp.where(height == rank * per + p, infl[f, :, l * LANE:(l + 1) * LANE], 0.0)
                 line = jnp.sum(line, axis=0, keepdims=True)
                 tile = jnp.where(row == (1 + f) * nl + l, jnp.broadcast_to(line, (SUB, LANE)), tile)
         starts.append(tile)
@@ -126,7 +135,14 @@
         halo_out[0, v] = low
         halo_out[1, v] = high
 
-    pl.semaphore_wait(barrier, 2 + (inner - 1) + (outer - 1))
+    @pl.when(owner)
+    def _():
+        pl.semaphore_wait(barrier, 2 + (inner - 1) + (outer - 1))
+
+    @pl.when(jnp.logical_not(owner))
+    def _():
+        pl.semaphore_wait(barrier, 2 + owners)
+
     halos = [
         pltpu.make_async_remote_copy(
             src_ref=halo_out.at[side],
@@ -200,38 +216,22 @@
     for f in range(fields):
         scatter(new_ref[f, nx - 1], 1 + f)
 
+    def remote(source, target, phase, slot, device):
+        return pltpu.make_async_remote_copy(
+            src_ref=source,
+            dst_ref=target,
+            send_sem=ex_send.at[phase],
+            recv_sem=ex_recv.at[slot],
+            device_id=(device, wid),
+            device_id_type=MESH,
+        )
+
     def part(ref, k):
-        return ref.at[pl.ds(pl.multiple_of(k * chunk, SUB), chunk), :]
-
-    def exchange(source_of, into, at, peers, phase):
-        for peer, device in peers:
-            pltpu.make_async_remote_copy(
-                src_ref=source_of(peer),
-                dst_ref=part(into, at),
-                send_sem=ex_send.at[phase],
-                recv_sem=ex_recv.at[phase],
-                device_id=(device, wid),
-                device_id_type=MESH,
-            ).start()
+        return ref.at[pl.ds(k * chunk if isinstance(k, int) else pl.multiple_of(k * chunk, SUB), chunk), :]
 
     def total(ref, count, phase):
         span = ref.at[pl.ds(0, count * chunk), :]
-        return pltpu.make_async_remote_copy(
-            src_ref=span,
-            dst_ref=span,
-            send_sem=ex_send.at[phase],
-            recv_sem=ex_recv.at[phase],
-            device_id=(me, right),
-            device_id_type=MESH,
-        )
-
-    group = [(group_peer(j), block * inner + group_peer(j)) for j in range(1, inner)]
-    blocks = [(block_peer(j), block_peer(j) * inner + mine) for j in range(1, outer)]
-
-    exchange(lambda k: part(send1, k), recv1, mine, group, 0)
-    own = pl.ds(pl.multiple_of(mine * chunk, SUB), chunk)
-    recv1[own, :] = send1[own, :]
-    total(recv1, inner - 1, 0).wait_recv()
+        return remote(span, span, phase, phase, me)
 
     def load_map(ref, at):
         tile = ref[at:at + SUB, :]
@@ -240,35 +240,61 @@
             decay = jnp.where(row % nl == l, jnp.broadcast_to(tile[l:l + 1], (SUB, LANE)), decay)
         return decay, tile
 
-    prefix = []
-    for p in range(per):
-        decay, state = jnp.ones((SUB, LANE), jnp.float32), jnp.zeros((SUB, LANE), jnp.float32)
-        line = []
+    for w in owner_order:
+        k = (w + shift) % inner
+
+        @pl.when(mine != k)
+        def _():
+            remote(part(send1, w), part(recv1, mine), 0, 0, block * inner + k).start()
+
+    @pl.when(owner)
+    def _():
+        own = pl.ds(pl.multiple_of(mine * chunk, SUB), chunk)
+        recv1[own, :] = send1[pl.ds(pl.multiple_of(rank * chunk, SUB), chunk), :]
+        total(recv1, inner - 1, 0).wait_recv()
+        prefix = []
+        for p in range(per):
+            decay, state = jnp.ones((SUB, LANE), jnp.float32), jnp.zeros((SUB, LANE), jnp.float32)
+            line = []
+            for k in range(inner):
+                line.append((decay, state))
+                d, s = load_map(recv1, k * chunk + p * SUB)
+                decay, state = d * decay, d * state + s
+            prefix.append(line)
+            send2[p * SUB:(p + 1) * SUB, :] = jnp.where(row < nl, decay, state)
+
+        for j in range(1, outer):
+            @pl.when(block + j < outer)
+            def _():
+                remote(send2, part(recv2, block), 1, 3 + block, (block + j) * inner + mine).start()
+
+        for b in range(outer - 1):
+            @pl.when(b < block)
+            def _():
+                remote(send2, part(recv2, b), 1, 3 + b, me).wait_recv()
+
+        for p in range(per):
+            entry = starts[p]
+            for b in range(outer - 1):
+                d, s = load_map(recv2, b * chunk + p * SUB)
+                entry = jnp.where(b < block, d * entry + s, entry)
+            for k in range(inner):
+                d, s = prefix[p][k]
+                send3[k * chunk + p * SUB:k * chunk + (p + 1) * SUB, :] = d * entry + s
+
         for k in range(inner):
-            line.append((decay, state))
-            d, s = load_map(recv1, k * chunk + p * SUB)
-            decay, state = d * decay, d * state + s
-        prefix.append(line)
-        send2[p * SUB:(p + 1) * SUB, :] = jnp.where(row < nl, decay, state)
-
-    if outer > 1:
-        exchange(lambda k: send2, recv2, block, blocks, 1)
-        own = pl.ds(pl.multiple_of(block * chunk, SUB), chunk)
-        recv2[own, :] = send2[...]
-        total(recv2, outer - 1, 1).wait_recv()
-    for p in range(per):
-        entry = starts[p]
-        for b in range(outer - 1):
-            d, s = load_map(recv2, b * chunk + p * SUB)
-            entry = jnp.where(b < block, d * entry + s, entry)
-        for k in range(inner):
-            d, s = prefix[p][k]
-            send3[k * chunk + p * SUB:k * chunk + (p + 1) * SUB, :] = d * entry + s
-
-    exchange(lambda k: part(send3, k), recv3, mine, group, 2)
-    own = pl.ds(pl.multiple_of(mine * chunk, SUB), chunk)
-    recv3[own, :] = send3[own, :]
-    total(recv3, inner - 1, 2).wait_recv()
+            @pl.when(mine != k)
+            def _():
+                remote(part(send3, k), part(recv3, rank), 2, 2, block * inner + k).start()
+
+        own = pl.ds(pl.multiple_of(rank * chunk, SUB), chunk)
+        recv3[own, :] = send3[pl.ds(pl.multiple_of(mine * chunk, SUB), chunk), :]
+        total(recv3, owners - 1, 2).wait_recv()
+
+    @pl.when(jnp.logical_not(owner))
+    def _():
+        total(recv3, owners, 2).wait_recv()
+
     for f in range(fields):
         for h in range(nh):
             for l in range(nl):
@@ -279,10 +305,30 @@
 
     for halo in halos:
         halo.wait_send()
-    total(send1, inner - 1, 0).wait_send()
-    if outer > 1:
-        total(recv2, outer - 1, 1).wait_send()
-    total(send3, inner - 1, 2).wait_send()
+
+    @pl.when(owner)
+    def _():
+        total(send1, owners - 1, 0).wait_send()
+        for j in range(1, outer):
+            @pl.when(block + j < outer)
+            def _():
+                remote(send2, send2, 1, 1, me).wait_send()
+        total(send3, inner - 1, 2).wait_send()
+
+    @pl.when(jnp.logical_not(owner))
+    def _():
+        total(send1, owners, 0).wait_send()
+
+
+def store_kernel(new_in, tend_in, new_out, tend_out, sem):
+    copies = [
+        pltpu.make_async_copy(src, dst, sem.at[i])
+        for i, (src, dst) in enumerate(((new_in, new_out), (tend_in, tend_out)))
+    ]
+    for copy in copies:
+        copy.start()
+    for copy in copies:
+        copy.wait()
 
 
 def shards(inner, flow_state, courant, inflow, height_ops, metric_index):
@@ -290,17 +336,22 @@
     count = lax.axis_size("len")
     nwid = lax.axis_size("wid")
     outer = count // inner
-    chunk = nz // inner * SUB
+    owners = inner // 2
+    chunk = nz // owners * SUB
     out = jax.ShapeDtypeStruct(flow_state.shape, jnp.float32)
     anywhere = pl.BlockSpec(memory_space=pl.ANY)
     nrow = fields * nx * (nz // SUB)
     npack = pl.cdiv(nrow, LANE // 4)
     f32 = jnp.float32
     dma = pltpu.SemaphoreType.DMA
-    return pl.pallas_call(
+    held = [
+        pltpu.with_memory_space_constraint(value, pltpu.HBM)
+        for value in (flow_state, courant, inflow, height_ops, metric_index)
+    ]
+    new_state, tendency = pl.pallas_call(
         functools.partial(sweep_kernel, inner, outer, nwid, metric_index.shape[0]),
         out_shape=(out, out),
-        in_specs=[anywhere] * 5,
+        in_specs=[pl.BlockSpec(memory_space=pltpu.HBM)] * 5,
         out_specs=(pl.BlockSpec(memory_space=pltpu.VMEM),) * 2,
         scratch_shapes=[
             pltpu.VMEM(flow_state.shape, f32),
@@ -311,21 +362,32 @@
             pltpu.VMEM(courant.shape, f32),
             pltpu.VMEM((2, npack, SUB, LANE), f32),
             pltpu.VMEM((2, npack, SUB, LANE), f32),
-            pltpu.VMEM((inner * chunk, LANE), f32),
+            pltpu.VMEM((owners * chunk, LANE), f32),
             pltpu.VMEM((inner * chunk, LANE), f32),
             pltpu.VMEM((chunk, LANE), f32),
             pltpu.VMEM((outer * chunk, LANE), f32),
             pltpu.VMEM((inner * chunk, LANE), f32),
-            pltpu.VMEM((inner * chunk, LANE), f32),
+            pltpu.VMEM((owners * chunk, LANE), f32),
             dma((5,)),
             dma((2,)),
             dma((2,)),
             dma((3,)),
-            dma((3,)),
+            dma((3 + outer,)),
         ],
-        compiler_params=pltpu.CompilerParams(collective_id=0, has_side_effects=True),
+        compiler_params=pltpu.CompilerParams(
+            collective_id=0, has_side_effects=True, vmem_limit_bytes=16 << 20
+        ),
         name="sweep",
-    )(flow_state, courant, inflow, height_ops, metric_index)
+    )(*held)
+    return pl.pallas_call(
+        store_kernel,
+        out_shape=(out, out),
+        in_specs=[anywhere] * 2,
+        out_specs=(anywhere, anywhere),
+        scratch_shapes=[dma((2,))],
+        compiler_params=pltpu.CompilerParams(vmem_limit_bytes=4 << 20),
+        name="finish",
+    )(new_state, tendency)
 
 
 def solution(mesh, inner=16):

time: 35.6 us -> 30.3 us (0.85)
  the two profiles are of different devices: /device:TPU:1 before, /device:TPU:7 now
where the time goes in v1:
time: 30.3 us; the launch traced here: 30.2 us
  Pallas kernels  29.6 us (98%)
  between operations  0.64 us (2%)
    pallas_call x1, Pallas kernels, shards(): pl.pallas_call(functools.partial(sweep_kernel, inner, outer, nwid, metric...  28.7 us
    pallas_call x1, Pallas kernels, shards(): pl.pallas_call(store_kernel, out_shape=(out, out), in_specs=[anywhere] *...  0.89 us

profile of v1, /device:TPU:7, one launch (start us, length us, event | category | flops | bytes accessed | tf_op | source)
XLA Modules:
  0.0 30.2 jit_solution(17073603429982715047)
XLA Ops:
  0.6 28.7 %sweep.1 = (f32[3,8,16,256]{3,2,1,0:T(8,128)S(1)}, f32[3,8,16,256]{3,2,1,0:T(8,128)S(1)}) custom-call(f32[3,8,16,256]{3,2,1,0:T(8,128)} %flow_hbm.1, f32[8,16,256]{2,1,0:T(8,128)} %cour_hbm.1, f32[3,16,256]{2,1,0:T(8,128)} %inflow_hbm.1, f32[8,16,16]{2,1,0:T(8,128)} %ops_hbm.1, s32[2]{0:T(128)} %metric_hbm.1), custom_call_target="tpu_custom_call" | custom-call | tf_op jit(solution)/shard_map/sweep/pallas_call | solution.py:351
  29.3 0.9 %finish.1 = (f32[3,8,16,256]{3,2,1,0:T(8,128)}, f32[3,8,16,256]{3,2,1,0:T(8,128)}) custom-call(f32[3,8,16,256]{3,2,1,0:T(8,128)S(1)} %get-tuple-element.4.new_in, f32[3,8,16,256]{3,2,1,0:T(8,128)S(1)} %get-tuple-element.5.tend_in), custom_call_target="tpu_custom_call" | custom-call | tf_op jit(solution)/shard_map/finish/pallas_call | solution.py:382

commit v2 on v1

v2 whole, which is shorter than its diff:
```python
import functools

import jax
import jax.numpy as jnp
from jax import lax
from jax.experimental import pallas as pl
from jax.experimental.pallas import tpu as pltpu
from jax.sharding import PartitionSpec as P

STEP = 0.25
SHIFT = 0
LANE = 128
SUB = 8
MESH = pl.DeviceIdType.MESH


def split_bf16(value):
    high = value.astype(jnp.bfloat16)
    return high, (value - high.astype(jnp.float32)).astype(jnp.bfloat16)


def sweep_kernel(
    inner, outer, deep, nwid, groups,
    flow_hbm, cour_hbm, inflow_hbm, ops_hbm, metric_hbm,
    new_ref, tend_ref,
    flow, cour, infl, ops, metric, prod, keep, gain, halo_out, halo_in,
    send1, recv1, send3, recv3,
    in_sem, halo_send, halo_recv, ex_send, ex_recv,
):
    fields, nx, nz, ny = flow.shape
    nh, nl = nz // SUB, ny // LANE
    count = inner * outer
    owners = deep * outer
    per = nz // owners
    chunk = per * SUB
    half = inner // 2
    me = lax.axis_index("len")
    wid = lax.axis_index("wid")
    mine = lax.rem(me, inner)
    block = lax.div(me, inner)
    right, left = lax.rem(wid + 1, nwid), lax.rem(wid + nwid - 1, nwid)

    loads = [
        pltpu.make_async_copy(src, dst, in_sem.at[i])
        for i, (src, dst) in enumerate(
            ((flow_hbm, flow), (cour_hbm, cour), (inflow_hbm, infl), (ops_hbm, ops), (metric_hbm, metric))
        )
    ]
    for load in loads:
        load.start()

    place = lax.rem(mine + (inner - SHIFT), inner)
    owner = place < deep
    rank = block + outer * place

    def seat(w):
        return (w % outer) * inner + (SHIFT + w // outer) % inner

    barrier = pltpu.get_barrier_semaphore()

    def greet(to, across):
        pl.semaphore_signal(barrier, inc=1, device_id=(to, across), device_id_type=MESH)

    greet(me, left)
    greet(me, right)
    seats = [seat(w) for w in range(owners)]
    for t in seats:
        @pl.when(me != t)
        def _():
            greet(t, wid)

    @pl.when(owner)
    def _():
        for t in range(count):
            if t not in seats:
                greet(t, wid)

    row = lax.broadcasted_iota(jnp.int32, (SUB, LANE), 0)
    lane = lax.broadcasted_iota(jnp.int32, (SUB, LANE), 1)
    slot, spot = lane // 4, lane % 4

    loads[0].wait()
    nrow = fields * nx * nh
    slots = LANE // 4
    npack = pl.cdiv(nrow, slots)

    def where_is(r):
        f, i, h = r // (nx * nh), (r // nh) % nx, r % nh
        return f, i, slice(h * SUB, (h + 1) * SUB)

    packed = []
    for v in range(npack):
        low = jnp.zeros((SUB, LANE), jnp.float32)
        high = low
        for s in range(min(slots, nrow - v * slots)):
            f, i, z = where_is(v * slots + s)
            here = slot == s
            first, last = flow[f, i, z, :LANE], flow[f, i, z, ny - LANE:]
            low = jnp.where(here, pltpu.roll(first, 4 * s, 1) if s else first, low)
            high = jnp.where(here, pltpu.roll(last, (4 * s + 3) % LANE, 1), high)
        low = jnp.where(spot < 3, low, 0.0)
        high = jnp.where(spot < 3, high, 0.0)
        packed.append((low, high))
        halo_out[0, v] = low
        halo_out[1, v] = high

    @pl.when(owner)
    def _():
        pl.semaphore_wait(barrier, 2 + count - 1)

    @pl.when(jnp.logical_not(owner))
    def _():
        pl.semaphore_wait(barrier, 2 + owners)

    halos = [
        pltpu.make_async_remote_copy(
            src_ref=halo_out.at[side],
            dst_ref=halo_in.at[side],
            send_sem=halo_send.at[side],
            recv_sem=halo_recv.at[side],
            device_id=(me, to),
            device_id_type=MESH,
        )
        for side, to in ((0, left), (1, right))
    ]
    for halo in halos:
        halo.start()

    loads[4].wait()
    loads[3].wait()
    rows = nx * nz
    tiles = []
    for g in range(groups):
        one = ops[metric[g]]
        tiles.append(jnp.concatenate([one] * nx, axis=1))
    row_cell = lax.broadcasted_iota(jnp.int32, (nz, rows), 1) // nz
    diag = jnp.concatenate(
        [jnp.where(row_cell == i, tiles[i * groups // nx], 0.0) for i in range(nx)], axis=0
    )
    diag_high, diag_low = split_bf16(diag)

    loads[1].wait()
    for i in range(nx):
        c = cour[i]
        t = 1.0 / (1.0 + c)
        cour[i] = t
        k = jnp.where(c < 1.0, c * t, 1.0 - t)
        keep[i] = k
        gain[i] = STEP * t * flow[1, i]
        prod[i] = k if i == 0 else k * prod[i - 1]

    loads[2].wait()
    height = lax.broadcasted_iota(jnp.int32, (nz, LANE), 0)
    starts = []
    for p in range(per):
        tile = jnp.zeros((SUB, LANE), jnp.float32)
        for f in range(fields):
            for l in range(nl):
                line = jnp.where(height == rank * per + p, infl[f, :, l * LANE:(l + 1) * LANE], 0.0)
                line = jnp.sum(line, axis=0, keepdims=True)
                tile = jnp.where(row == (1 + f) * nl + l, jnp.broadcast_to(line, (SUB, LANE)), tile)
        starts.append(tile)

    for f in range(fields):
        q = flow[f].reshape(rows, ny)
        q_high, q_low = split_bf16(q)
        vertical = jnp.dot(diag_high, q_high, preferred_element_type=jnp.float32)
        vertical += jnp.dot(diag_low, q_high, preferred_element_type=jnp.float32)
        vertical += jnp.dot(diag_high, q_low, preferred_element_type=jnp.float32)
        for i in range(nx):
            q = flow[f, i]
            slopes = jnp.zeros((nz, ny), jnp.float32)
            for offset, factor in ((1, 45.0 / 60.0), (2, -9.0 / 60.0), (3, 1.0 / 60.0)):
                slopes += factor * (pltpu.roll(q, ny - offset, 1) - pltpu.roll(q, offset, 1))
            tend = vertical[i * nz:(i + 1) * nz] - flow[1, i] * slopes
            tend_ref[f, i] = tend
            new_ref[f, i] = cour[i] * (q + STEP * tend)

    for halo in halos:
        halo.wait_recv()
    fixes = []
    for v in range(npack):
        low, high = packed[v]
        before = jnp.where(wid == 0, 0.0, halo_in[1, v]) - high
        after = jnp.where(wid == nwid - 1, 0.0, halo_in[0, v]) - low
        fix_low = (
            (-1.0 / 60.0) * before
            + jnp.where(spot < 2, 9.0 / 60.0, 0.0) * pltpu.roll(before, LANE - 1, 1)
            + jnp.where(spot < 1, -45.0 / 60.0, 0.0) * pltpu.roll(before, LANE - 2, 1)
        )
        fix_high = (
            (1.0 / 60.0) * after
            + jnp.where(spot >= 1, -9.0 / 60.0, 0.0) * pltpu.roll(after, 1, 1)
            + jnp.where(spot >= 2, 45.0 / 60.0, 0.0) * pltpu.roll(after, 2, 1)
        )
        fixes.append((fix_low, fix_high))

    def scatter(tile, v, h, l):
        send1[pl.ds(h * SUB * SUB + v * nl + l, SUB, stride=SUB), :] = tile

    for h in range(nh):
        z = slice(h * SUB, (h + 1) * SUB)
        for l in range(nl):
            y = slice(l * LANE, (l + 1) * LANE)
            scatter(prod[nx - 1, z, y], 0, h, l)
            for f in range(fields):
                state = None
                for i in range(nx):
                    v, s = divmod((f * nx + i) * nh + h, slots)
                    more = new_ref[f, i, z, y]
                    if l == 0 or l == nl - 1:
                        fix = jnp.zeros((SUB, LANE), jnp.float32)
                        if l == 0:
                            turned = pltpu.roll(fixes[v][0], LANE - 4 * s, 1) if s else fixes[v][0]
                            fix = jnp.where(lane < 3, turned, fix)
                        if l == nl - 1:
                            turned = pltpu.roll(fixes[v][1], (2 * LANE - 3 - 4 * s) % LANE, 1)
                            fix = jnp.where(lane >= LANE - 3, turned, fix)
                        tend_ref[f, i, z, y] -= flow[1, i, z, y] * fix
                        more -= gain[i, z, y] * fix
                    state = more if state is None else keep[i, z, y] * state + more
                    new_ref[f, i, z, y] = state
                scatter(state, 1 + f, h, l)

    def remote(source, target, phase, slot, device):
        return pltpu.make_async_remote_copy(
            src_ref=source,
            dst_ref=target,
            send_sem=ex_send.at[phase],
            recv_sem=ex_recv.at[slot],
            device_id=(device, wid),
            device_id_type=MESH,
        )

    def rows_of(k):
        return pl.ds(k * chunk if isinstance(k, int) else pl.multiple_of(k * chunk, SUB), chunk)

    def part(ref, k):
        return ref.at[rows_of(k), :]

    def total(ref, parts, phase, slot):
        span = ref.at[pl.ds(0, parts * chunk), :]
        return remote(span, span, phase, slot, me)

    def load_map(ref, at):
        tile = ref[at:at + SUB, :]
        decay = jnp.broadcast_to(tile[0:1], (SUB, LANE))
        for l in range(1, nl):
            decay = jnp.where(row % nl == l, jnp.broadcast_to(tile[l:l + 1], (SUB, LANE)), decay)
        return decay, tile

    section = lax.div(me, half)
    sections = 2 * outer
    back = sections
    for j in sorted(range(outer), key=lambda j: -min(j, outer - j)):
        to = lax.rem(block + j, outer)
        for r in range(deep):
            k = (SHIFT + r) % inner

            def give():
                remote(part(send1, to + outer * r), part(recv1, me), 0, section, to * inner + k).start()

            if j:
                give()
            else:
                pl.when(mine != k)(give)

    @pl.when(owner)
    def _():
        recv1[rows_of(me), :] = send1[rows_of(rank), :]
        entries = list(starts)

        def send_back(q):
            for t in range(q * half, (q + 1) * half):
                @pl.when(me != t)
                def _():
                    remote(part(send3, t), part(recv3, rank), 1, back, t).start()

        for q in range(sections):
            @pl.when(section == q)
            def _():
                total(recv1, half - 1, 0, q).wait_recv()

            @pl.when(section != q)
            def _():
                total(recv1, half, 0, q).wait_recv()

            for t in range(q * half, (q + 1) * half):
                for p in range(per):
                    at = t * chunk + p * SUB
                    send3[at:at + SUB, :] = entries[p]
                    decay, state = load_map(recv1, at)
                    entries[p] = decay * entries[p] + state
            if q % 2 == 0:
                send_back(q)
                if q:
                    send_back(q - 1)
        send_back(sections - 1)
        recv3[rows_of(rank), :] = send3[rows_of(me), :]
        total(recv3, owners - 1, 1, back).wait_recv()

    @pl.when(jnp.logical_not(owner))
    def _():
        total(recv3, owners, 1, back).wait_recv()

    for f in range(fields):
        for h in range(nh):
            for l in range(nl):
                enter = recv3[pl.ds(h * SUB * SUB + (1 + f) * nl + l, SUB, stride=SUB), :]
                z, y = slice(h * SUB, (h + 1) * SUB), slice(l * LANE, (l + 1) * LANE)
                for i in range(nx):
                    new_ref[f, i, z, y] += prod[i, z, y] * enter

    for halo in halos:
        halo.wait_send()

    @pl.when(owner)
    def _():
        total(send1, owners - 1, 0, 0).wait_send()
        total(send3, count - 1, 1, 0).wait_send()

    @pl.when(jnp.logical_not(owner))
    def _():
        total(send1, owners, 0, 0).wait_send()


def store_kernel(new_in, tend_in, new_out, tend_out, sem):
    copies = [
        pltpu.make_async_copy(src, dst, sem.at[i])
        for i, (src, dst) in enumerate(((new_in, new_out), (tend_in, tend_out)))
    ]
    for copy in copies:
        copy.start()
    for copy in copies:
        copy.wait()


def shards(inner, deep, flow_state, courant, inflow, height_ops, metric_index):
    fields, nx, nz, ny = flow_state.shape
    count = lax.axis_size("len")
    nwid = lax.axis_size("wid")
    outer = count // inner
    owners = deep * outer
    chunk = nz // owners * SUB
    out = jax.ShapeDtypeStruct(flow_state.shape, jnp.float32)
    anywhere = pl.BlockSpec(memory_space=pl.ANY)
    nrow = fields * nx * (nz // SUB)
    npack = pl.cdiv(nrow, LANE // 4)
    f32 = jnp.float32
    dma = pltpu.SemaphoreType.DMA
    held = [
        pltpu.with_memory_space_constraint(value, pltpu.HBM)
        for value in (flow_state, courant, inflow, height_ops, metric_index)
    ]
    new_state, tendency = pl.pallas_call(
        functools.partial(sweep_kernel, inner, outer, deep, nwid, metric_index.shape[0]),
        out_shape=(out, out),
        in_specs=[pl.BlockSpec(memory_space=pltpu.HBM)] * 5,
        out_specs=(pl.BlockSpec(memory_space=pltpu.VMEM),) * 2,
        scratch_shapes=[
            pltpu.VMEM(flow_state.shape, f32),
            pltpu.VMEM(courant.shape, f32),
            pltpu.VMEM(inflow.shape, f32),
            pltpu.VMEM(height_ops.shape, f32),
            pltpu.SMEM(metric_index.shape, jnp.int32),
            pltpu.VMEM(courant.shape, f32),
            pltpu.VMEM(courant.shape, f32),
            pltpu.VMEM(courant.shape, f32),
            pltpu.VMEM((2, npack, SUB, LANE), f32),
            pltpu.VMEM((2, npack, SUB, LANE), f32),
            pltpu.VMEM((owners * chunk, LANE), f32),
            pltpu.VMEM((count * chunk, LANE), f32),
            pltpu.VMEM((count * chunk, LANE), f32),
            pltpu.VMEM((owners * chunk, LANE), f32),
            dma((5,)),
            dma((2,)),
            dma((2,)),
            dma((2,)),
            dma((2 * outer + 1,)),
        ],
        compiler_params=pltpu.CompilerParams(
            collective_id=0, has_side_effects=True, vmem_limit_bytes=16 << 20
        ),
        name="sweep",
    )(*held)
    return pl.pallas_call(
        store_kernel,
        out_shape=(out, out),
        in_specs=[anywhere] * 2,
        out_specs=(anywhere, anywhere),
        scratch_shapes=[dma((2,))],
        compiler_params=pltpu.CompilerParams(vmem_limit_bytes=4 << 20),
        name="finish",
    )(new_state, tendency)


def solution(mesh, inner=16, deep=4):
    placed = (
        P(None, "len", None, "wid"),
        P("len", None, "wid"),
        P(None, None, "wid"),
        P(),
        P("len"),
    )
    return jax.shard_map(
        functools.partial(shards, inner, deep),
        mesh=mesh,
        in_specs=placed,
        out_specs=(P(None, "len", None, "wid"), P(None, "len", None, "wid")),
        check_vma=False,
    )
```

time: 30.3 us -> 28.5 us (0.941)
  the two profiles are of different devices: /device:TPU:7 before, /device:TPU:1 now
where the time goes in v2:
time: 28.5 us; the launch traced here: 28.4 us
  Pallas kernels  27.7 us (97%)
  between operations  0.64 us (2%)
    pallas_call x1, Pallas kernels, shards(): pl.pallas_call(functools.partial(sweep_kernel, inner, outer, deep, nwid,...  26.8 us
    pallas_call x1, Pallas kernels, shards(): pl.pallas_call(store_kernel, out_shape=(out, out), in_specs=[anywhere] *...  0.89 us

profile of v2, /device:TPU:1, one launch (start us, length us, event | category | flops | bytes accessed | tf_op | source)
XLA Modules:
  0.0 28.4 jit_solution(16344073091310392168)
XLA Ops:
  0.6 26.8 %sweep.1 = (f32[3,8,16,256]{3,2,1,0:T(8,128)S(1)}, f32[3,8,16,256]{3,2,1,0:T(8,128)S(1)}) custom-call(f32[3,8,16,256]{3,2,1,0:T(8,128)} %flow_hbm.1, f32[8,16,256]{2,1,0:T(8,128)} %cour_hbm.1, f32[3,16,256]{2,1,0:T(8,128)} %inflow_hbm.1, f32[8,16,16]{2,1,0:T(8,128)} %ops_hbm.1, s32[2]{0:T(128)} %metric_hbm.1), custom_call_target="tpu_custom_call" | custom-call | tf_op jit(solution)/shard_map/sweep/pallas_call | solution.py:355
  27.5 0.9 %finish.1 = (f32[3,8,16,256]{3,2,1,0:T(8,128)}, f32[3,8,16,256]{3,2,1,0:T(8,128)}) custom-call(f32[3,8,16,256]{3,2,1,0:T(8,128)S(1)} %get-tuple-element.4.new_in, f32[3,8,16,256]{3,2,1,0:T(8,128)S(1)} %get-tuple-element.5.tend_in), custom_call_target="tpu_custom_call" | custom-call | tf_op jit(solution)/shard_map/finish/pallas_call | solution.py:386

commit v3 on v2

--- a/solution.py
+++ b/solution.py
@@ -24,8 +24,9 @@
     flow_hbm, cour_hbm, inflow_hbm, ops_hbm, metric_hbm,
     new_ref, tend_ref,
     flow, cour, infl, ops, metric, prod, keep, gain, halo_out, halo_in,
+    edge_out, edge_in, pull_out, pull_in, edge_tiles,
     send1, recv1, send3, recv3,
-    in_sem, halo_send, halo_recv, ex_send, ex_recv,
+    in_sem, halo_send, halo_recv, edge_send, edge_recv, pull_send, pull_recv, ex_send, ex_recv,
 ):
     fields, nx, nz, ny = flow.shape
     nh, nl = nz // SUB, ny // LANE
@@ -74,43 +75,61 @@
         for t in range(count):
             if t not in seats:
                 greet(t, wid)
+            greet(t, left)
+            greet(t, right)
 
     row = lax.broadcasted_iota(jnp.int32, (SUB, LANE), 0)
     lane = lax.broadcasted_iota(jnp.int32, (SUB, LANE), 1)
     slot, spot = lane // 4, lane % 4
+    section = lax.div(me, half)
+    sections = 2 * outer
+    field_lanes = nx * 4
+    states = fields * nl
+    back_rows = per * states
+
+    ahead = lax.broadcasted_iota(jnp.int32, (ny, ny), 0) - lax.broadcasted_iota(jnp.int32, (ny, ny), 1)
+    reach = jnp.abs(ahead)
+    band = jnp.where(reach == 1, 45.0, jnp.where(reach == 2, -9.0, jnp.where(reach == 3, 1.0, 0.0)))
+    band = jnp.where(ahead < 0, -band, band).astype(jnp.bfloat16)
 
     loads[0].wait()
-    nrow = fields * nx * nh
-    slots = LANE // 4
-    npack = pl.cdiv(nrow, slots)
-
-    def where_is(r):
-        f, i, h = r // (nx * nh), (r // nh) % nx, r % nh
-        return f, i, slice(h * SUB, (h + 1) * SUB)
-
-    packed = []
-    for v in range(npack):
+    for h in range(nh):
+        z = slice(h * SUB, (h + 1) * SUB)
         low = jnp.zeros((SUB, LANE), jnp.float32)
         high = low
-        for s in range(min(slots, nrow - v * slots)):
-            f, i, z = where_is(v * slots + s)
-            here = slot == s
-            first, last = flow[f, i, z, :LANE], flow[f, i, z, ny - LANE:]
-            low = jnp.where(here, pltpu.roll(first, 4 * s, 1) if s else first, low)
-            high = jnp.where(here, pltpu.roll(last, (4 * s + 3) % LANE, 1), high)
+        for f in range(fields):
+            for i in range(nx):
+                s = f * nx + i
+                here = slot == s
+                first, last = flow[f, i, z, :LANE], flow[f, i, z, ny - LANE:]
+                low = jnp.where(here, pltpu.roll(first, 4 * s, 1) if s else first, low)
+                high = jnp.where(here, pltpu.roll(last, (4 * s + 3) % LANE, 1), high)
         low = jnp.where(spot < 3, low, 0.0)
         high = jnp.where(spot < 3, high, 0.0)
-        packed.append((low, high))
-        halo_out[0, v] = low
-        halo_out[1, v] = high
+        first = (
+            (1.0 / 60.0) * low
+            + jnp.where(spot >= 1, -9.0 / 60.0, 0.0) * pltpu.roll(low, 1, 1)
+            + jnp.where(spot >= 2, 45.0 / 60.0, 0.0) * pltpu.roll(low, 2, 1)
+        )
+        last = (
+            (-1.0 / 60.0) * high
+            + jnp.where(spot < 2, 9.0 / 60.0, 0.0) * pltpu.roll(high, LANE - 1, 1)
+            + jnp.where(spot < 1, -45.0 / 60.0, 0.0) * pltpu.roll(high, LANE - 2, 1)
+        )
+        first = jnp.where(spot < 3, first, 0.0)
+        last = jnp.where(spot < 3, last, 0.0)
+        halo_out[0, h] = first
+        halo_out[1, h] = last
+        edge_out[h * SUB:(h + 1) * SUB, 0, :] = first
+        edge_out[nz + h * SUB:nz + (h + 1) * SUB, 0, :] = last
 
     @pl.when(owner)
     def _():
-        pl.semaphore_wait(barrier, 2 + count - 1)
+        pl.semaphore_wait(barrier, 2 + count - 1 + 2 * owners)
 
     @pl.when(jnp.logical_not(owner))
     def _():
-        pl.semaphore_wait(barrier, 2 + owners)
+        pl.semaphore_wait(barrier, 2 + 3 * owners)
 
     halos = [
         pltpu.make_async_remote_copy(
@@ -123,6 +142,28 @@
         )
         for side, to in ((0, left), (1, right))
     ]
+    def far_first(act):
+        for j in sorted(range(outer), key=lambda j: -min(j, outer - j)):
+            to = lax.rem(block + j, outer)
+            for r in range(deep):
+                act(j, to + outer * r, to * inner + (SHIFT + r) % inner)
+
+    def edge_copy(side, across, w, device, p):
+        return pltpu.make_async_remote_copy(
+            src_ref=edge_out.at[pl.ds(side * nz + w * per + p, 1)],
+            dst_ref=edge_in.at[pl.ds(((1 - side) * per + p) * count + me, 1)],
+            send_sem=edge_send,
+            recv_sem=edge_recv.at[section],
+            device_id=(device, across),
+            device_id_type=MESH,
+        )
+
+    def give_edges(j, w, device):
+        for p in range(per):
+            edge_copy(0, left, w, device, p).start()
+            edge_copy(1, right, w, device, p).start()
+
+    far_first(give_edges)
     for halo in halos:
         halo.start()
 
@@ -149,6 +190,69 @@
         gain[i] = STEP * t * flow[1, i]
         prod[i] = k if i == 0 else k * prod[i - 1]
 
+    pulls = []
+    after = None
+    tiles = [jnp.zeros((SUB, LANE), jnp.float32) for _ in range(nh)]
+    for i in reversed(range(nx)):
+        weight = -gain[i] if after is None else -gain[i] * after
+        after = keep[i] if after is None else after * keep[i]
+        for h in range(nh):
+            z = slice(h * SUB, (h + 1) * SUB)
+            turned = pltpu.roll(weight[z, :LANE], 4 * i, 1) if i else weight[z, :LANE]
+            tiles[h] = jnp.where(slot == i, turned, tiles[h])
+            turned = pltpu.roll(weight[z, ny - LANE:], (4 * (nx + i) + 3) % LANE, 1)
+            tiles[h] = jnp.where(slot == nx + i, turned, tiles[h])
+    for h in range(nh):
+        pulls.append(jnp.where(spot < 3, tiles[h], 0.0))
+        pull_out[h * SUB:(h + 1) * SUB, 0, :] = pulls[h]
+
+    def pull_copy(w, device, p):
+        return pltpu.make_async_remote_copy(
+            src_ref=pull_out.at[pl.ds(w * per + p, 1)],
+            dst_ref=pull_in.at[pl.ds(p * count + me, 1)],
+            send_sem=pull_send,
+            recv_sem=pull_recv.at[section],
+            device_id=(device, wid),
+            device_id_type=MESH,
+        )
+
+    def give_pulls(j, w, device):
+        def give():
+            for p in range(per):
+                pull_copy(w, device, p).start()
+
+        if j:
+            give()
+        else:
+            pl.when(me != device)(give)
+
+    far_first(give_pulls)
+
+    def edge_terms(at_start, at_end, pull):
+        lanes = lax.broadcasted_iota(jnp.int32, pull.shape, 1)
+
+        def summed(edges, weights):
+            spread = weights
+            for f in range(1, fields):
+                spread = spread + pltpu.roll(weights, f * field_lanes, 1)
+            value = edges * spread
+            step = field_lanes // 2
+            while step >= 4:
+                value = value + pltpu.roll(value, LANE - step, 1)
+                step //= 2
+            return value
+
+        begin = summed(at_start, jnp.where(lanes < field_lanes, pull, 0.0))
+        moved = pltpu.roll(pull, LANE - field_lanes, 1)
+        end = summed(at_end, jnp.where(lanes < field_lanes, moved, 0.0))
+        terms = []
+        for f in range(fields):
+            turned = pltpu.roll(begin, LANE - f * field_lanes, 1) if f else begin
+            first = jnp.where(lanes < 3, turned, 0.0)
+            turned = pltpu.roll(end, (2 * LANE - 3 - f * field_lanes) % LANE, 1)
+            terms.append((first, jnp.where(lanes >= LANE - 3, turned, 0.0)))
+        return terms
+
     loads[2].wait()
     height = lax.broadcasted_iota(jnp.int32, (nz, LANE), 0)
     starts = []
@@ -158,42 +262,21 @@
             for l in range(nl):
                 line = jnp.where(height == rank * per + p, infl[f, :, l * LANE:(l + 1) * LANE], 0.0)
                 line = jnp.sum(line, axis=0, keepdims=True)
-                tile = jnp.where(row == (1 + f) * nl + l, jnp.broadcast_to(line, (SUB, LANE)), tile)
+                tile = jnp.where(row == f * nl + l, jnp.broadcast_to(line, (SUB, LANE)), tile)
         starts.append(tile)
 
     for f in range(fields):
-        q = flow[f].reshape(rows, ny)
-        q_high, q_low = split_bf16(q)
+        q_high, q_low = split_bf16(flow[f].reshape(rows, ny))
         vertical = jnp.dot(diag_high, q_high, preferred_element_type=jnp.float32)
         vertical += jnp.dot(diag_low, q_high, preferred_element_type=jnp.float32)
         vertical += jnp.dot(diag_high, q_low, preferred_element_type=jnp.float32)
+        slopes = jnp.dot(q_high, band, preferred_element_type=jnp.float32)
+        slopes += jnp.dot(q_low, band, preferred_element_type=jnp.float32)
         for i in range(nx):
-            q = flow[f, i]
-            slopes = jnp.zeros((nz, ny), jnp.float32)
-            for offset, factor in ((1, 45.0 / 60.0), (2, -9.0 / 60.0), (3, 1.0 / 60.0)):
-                slopes += factor * (pltpu.roll(q, ny - offset, 1) - pltpu.roll(q, offset, 1))
-            tend = vertical[i * nz:(i + 1) * nz] - flow[1, i] * slopes
+            at = slice(i * nz, (i + 1) * nz)
+            tend = vertical[at] - flow[1, i] * ((1.0 / 60.0) * slopes[at])
             tend_ref[f, i] = tend
-            new_ref[f, i] = cour[i] * (q + STEP * tend)
-
-    for halo in halos:
-        halo.wait_recv()
-    fixes = []
-    for v in range(npack):
-        low, high = packed[v]
-        before = jnp.where(wid == 0, 0.0, halo_in[1, v]) - high
-        after = jnp.where(wid == nwid - 1, 0.0, halo_in[0, v]) - low
-        fix_low = (
-            (-1.0 / 60.0) * before
-            + jnp.where(spot < 2, 9.0 / 60.0, 0.0) * pltpu.roll(before, LANE - 1, 1)
-            + jnp.where(spot < 1, -45.0 / 60.0, 0.0) * pltpu.roll(before, LANE - 2, 1)
-        )
-        fix_high = (
-            (1.0 / 60.0) * after
-            + jnp.where(spot >= 1, -9.0 / 60.0, 0.0) * pltpu.roll(after, 1, 1)
-            + jnp.where(spot >= 2, 45.0 / 60.0, 0.0) * pltpu.roll(after, 2, 1)
-        )
-        fixes.append((fix_low, fix_high))
+            new_ref[f, i] = cour[i] * (flow[f, i] + STEP * tend)
 
     def scatter(tile, v, h, l):
         send1[pl.ds(h * SUB * SUB + v * nl + l, SUB, stride=SUB), :] = tile
@@ -202,25 +285,14 @@
         z = slice(h * SUB, (h + 1) * SUB)
         for l in range(nl):
             y = slice(l * LANE, (l + 1) * LANE)
-            scatter(prod[nx - 1, z, y], 0, h, l)
+            scatter(prod[nx - 1, z, y], fields, h, l)
             for f in range(fields):
                 state = None
                 for i in range(nx):
-                    v, s = divmod((f * nx + i) * nh + h, slots)
                     more = new_ref[f, i, z, y]
-                    if l == 0 or l == nl - 1:
-                        fix = jnp.zeros((SUB, LANE), jnp.float32)
-                        if l == 0:
-                            turned = pltpu.roll(fixes[v][0], LANE - 4 * s, 1) if s else fixes[v][0]
-                            fix = jnp.where(lane < 3, turned, fix)
-                        if l == nl - 1:
-                            turned = pltpu.roll(fixes[v][1], (2 * LANE - 3 - 4 * s) % LANE, 1)
-                            fix = jnp.where(lane >= LANE - 3, turned, fix)
-                        tend_ref[f, i, z, y] -= flow[1, i, z, y] * fix
-                        more -= gain[i, z, y] * fix
                     state = more if state is None else keep[i, z, y] * state + more
                     new_ref[f, i, z, y] = state
-                scatter(state, 1 + f, h, l)
+                scatter(state, f, h, l)
 
     def remote(source, target, phase, slot, device):
         return pltpu.make_async_remote_copy(
@@ -244,83 +316,165 @@
 
     def load_map(ref, at):
         tile = ref[at:at + SUB, :]
-        decay = jnp.broadcast_to(tile[0:1], (SUB, LANE))
+        decay = jnp.broadcast_to(tile[states:states + 1], (SUB, LANE))
         for l in range(1, nl):
-            decay = jnp.where(row % nl == l, jnp.broadcast_to(tile[l:l + 1], (SUB, LANE)), decay)
+            decay = jnp.where(row % nl == l, jnp.broadcast_to(tile[states + l:states + l + 1], (SUB, LANE)), decay)
         return decay, tile
 
-    section = lax.div(me, half)
-    sections = 2 * outer
     back = sections
-    for j in sorted(range(outer), key=lambda j: -min(j, outer - j)):
-        to = lax.rem(block + j, outer)
-        for r in range(deep):
-            k = (SHIFT + r) % inner
-
-            def give():
-                remote(part(send1, to + outer * r), part(recv1, me), 0, section, to * inner + k).start()
-
-            if j:
-                give()
-            else:
-                pl.when(mine != k)(give)
+
+    def back_part(ref, k):
+        return ref.at[pl.ds(k * back_rows, back_rows)]
+
+    def back_total(ref, parts):
+        span = ref.at[pl.ds(0, parts * back_rows)]
+        return remote(span, span, 1, back, me)
+
+    def give_map(j, w, device):
+        def give():
+            remote(part(send1, w), part(recv1, me), 0, section, device).start()
+
+        if j:
+            give()
+        else:
+            pl.when(me != device)(give)
+
+    far_first(give_map)
+
+    for halo in halos:
+        halo.wait_recv()
+    for h in range(nh):
+        z = slice(h * SUB, (h + 1) * SUB)
+        fix_start = jnp.where(wid == 0, 0.0, halo_in[1, h])
+        fix_end = jnp.where(wid == nwid - 1, 0.0, halo_in[0, h])
+        for l in {0, nl - 1}:
+            y = slice(l * LANE, (l + 1) * LANE)
+            for f in range(fields):
+                state = None
+                for i in range(nx):
+                    s = f * nx + i
+                    fix = jnp.zeros((SUB, LANE), jnp.float32)
+                    if l == 0:
+                        turned = pltpu.roll(fix_start, LANE - 4 * s, 1) if s else fix_start
+                        fix = jnp.where(lane < 3, turned, fix)
+                    if l == nl - 1:
+                        turned = pltpu.roll(fix_end, (2 * LANE - 3 - 4 * s) % LANE, 1)
+                        fix = jnp.where(lane >= LANE - 3, turned, fix)
+                    tend_ref[f, i, z, y] -= flow[1, i, z, y] * fix
+                    more = gain[i, z, y] * fix
+                    state = more if state is None else keep[i, z, y] * state + more
+                    new_ref[f, i, z, y] -= state
 
     @pl.when(owner)
     def _():
         recv1[rows_of(me), :] = send1[rows_of(rank), :]
+        for p in range(per):
+            pull_in[pl.ds(p * count + me, 1)] = pull_out[pl.ds(rank * per + p, 1)]
+
+        def pull_wait(parts, q):
+            span = pull_in.at[pl.ds(0, parts * per)]
+            pltpu.make_async_remote_copy(
+                src_ref=span, dst_ref=span, send_sem=pull_send, recv_sem=pull_recv.at[q],
+                device_id=(me, right), device_id_type=MESH,
+            ).wait_recv()
+
         entries = list(starts)
 
         def send_back(q):
             for t in range(q * half, (q + 1) * half):
-                @pl.when(me != t)
-                def _():
-                    remote(part(send3, t), part(recv3, rank), 1, back, t).start()
+                def give():
+                    remote(back_part(send3, t), back_part(recv3, rank), 1, back, t).start()
+
+                if t in seats:
+                    pl.when(me != t)(give)
+                else:
+                    give()
 
         for q in range(sections):
             @pl.when(section == q)
             def _():
+                pull_wait(half - 1, q)
                 total(recv1, half - 1, 0, q).wait_recv()
 
             @pl.when(section != q)
             def _():
+                pull_wait(half, q)
                 total(recv1, half, 0, q).wait_recv()
+
+            span = edge_in.at[pl.ds(0, 2 * half * per)]
+            pltpu.make_async_remote_copy(
+                src_ref=span, dst_ref=span, send_sem=edge_send, recv_sem=edge_recv.at[q],
+                device_id=(me, right), device_id_type=MESH,
+            ).wait_recv()
+            for p in range(per):
+                at = p * count + q * half
+                terms = edge_terms(
+                    jnp.where(wid == 0, 0.0, edge_in[at:at + half, 0, :]),
+                    jnp.where(wid == nwid - 1, 0.0, edge_in[per * count + at:per * count + at + half, 0, :]),
+                    pull_in[at:at + half, 0, :],
+                )
+                for f in range(fields):
+                    for l in range(nl):
+                        term = jnp.zeros((half, LANE), jnp.float32)
+                        if l == 0:
+                            term += terms[f][0]
+                        if l == nl - 1:
+                            term += terms[f][1]
+                        edge_tiles[pl.ds(at * SUB + f * nl + l, half, stride=SUB), :] = term
 
             for t in range(q * half, (q + 1) * half):
                 for p in range(per):
                     at = t * chunk + p * SUB
-                    send3[at:at + SUB, :] = entries[p]
+                    send3[t * back_rows + p * states:t * back_rows + (p + 1) * states, 0, :] = entries[p][:states]
                     decay, state = load_map(recv1, at)
-                    entries[p] = decay * entries[p] + state
+                    edge = edge_tiles[(p * count + t) * SUB:(p * count + t + 1) * SUB, :]
+                    edge = jnp.where(row < states, edge, 0.0)
+                    entries[p] = decay * entries[p] + (state + edge)
             if q % 2 == 0:
                 send_back(q)
-                if q:
-                    send_back(q - 1)
+                if q > 2:
+                    send_back(q - 3)
+        send_back(sections - 3)
         send_back(sections - 1)
-        recv3[rows_of(rank), :] = send3[rows_of(me), :]
-        total(recv3, owners - 1, 1, back).wait_recv()
+        recv3[pl.ds(rank * back_rows, back_rows)] = send3[pl.ds(me * back_rows, back_rows)]
+        back_total(recv3, owners - 1).wait_recv()
 
     @pl.when(jnp.logical_not(owner))
     def _():
-        total(recv3, owners, 1, back).wait_recv()
+        back_total(recv3, owners).wait_recv()
 
     for f in range(fields):
         for h in range(nh):
             for l in range(nl):
-                enter = recv3[pl.ds(h * SUB * SUB + (1 + f) * nl + l, SUB, stride=SUB), :]
+                enter = recv3[pl.ds(h * SUB * states + f * nl + l, SUB, stride=states), 0, :]
                 z, y = slice(h * SUB, (h + 1) * SUB), slice(l * LANE, (l + 1) * LANE)
                 for i in range(nx):
                     new_ref[f, i, z, y] += prod[i, z, y] * enter
 
     for halo in halos:
         halo.wait_send()
+    span = edge_in.at[pl.ds(0, 2 * owners * per)]
+    pltpu.make_async_remote_copy(
+        src_ref=span, dst_ref=span, send_sem=edge_send, recv_sem=edge_recv.at[0],
+        device_id=(me, right), device_id_type=MESH,
+    ).wait_send()
+
+    def pull_sent(parts):
+        span = pull_in.at[pl.ds(0, parts * per)]
+        pltpu.make_async_remote_copy(
+            src_ref=span, dst_ref=span, send_sem=pull_send, recv_sem=pull_recv.at[0],
+            device_id=(me, right), device_id_type=MESH,
+        ).wait_send()
 
     @pl.when(owner)
     def _():
+        pull_sent(owners - 1)
         total(send1, owners - 1, 0, 0).wait_send()
-        total(send3, count - 1, 1, 0).wait_send()
+        back_total(send3, count - 1).wait_send()
 
     @pl.when(jnp.logical_not(owner))
     def _():
+        pull_sent(owners)
         total(send1, owners, 0, 0).wait_send()
 
 
@@ -344,8 +498,9 @@
     chunk = nz // owners * SUB
     out = jax.ShapeDtypeStruct(flow_state.shape, jnp.float32)
     anywhere = pl.BlockSpec(memory_space=pl.ANY)
-    nrow = fields * nx * (nz // SUB)
-    npack = pl.cdiv(nrow, LANE // 4)
+    nh = nz // SUB
+    states = fields * (ny // LANE)
+    heights = nz // owners * count
     f32 = jnp.float32
     dma = pltpu.SemaphoreType.DMA
     held = [
@@ -366,15 +521,24 @@
             pltpu.VMEM(courant.shape, f32),
             pltpu.VMEM(courant.shape, f32),
             pltpu.VMEM(courant.shape, f32),
-            pltpu.VMEM((2, npack, SUB, LANE), f32),
-            pltpu.VMEM((2, npack, SUB, LANE), f32),
+            pltpu.VMEM((2, nh, SUB, LANE), f32),
+            pltpu.VMEM((2, nh, SUB, LANE), f32),
+            pltpu.VMEM((2 * nz, 1, LANE), f32),
+            pltpu.VMEM((2 * heights, 1, LANE), f32),
+            pltpu.VMEM((nz, 1, LANE), f32),
+            pltpu.VMEM((heights, 1, LANE), f32),
+            pltpu.VMEM((heights * SUB, LANE), f32),
             pltpu.VMEM((owners * chunk, LANE), f32),
             pltpu.VMEM((count * chunk, LANE), f32),
-            pltpu.VMEM((count * chunk, LANE), f32),
-            pltpu.VMEM((owners * chunk, LANE), f32),
+            pltpu.VMEM((heights * states, 1, LANE), f32),
+            pltpu.VMEM((nz * states, 1, LANE), f32),
             dma((5,)),
             dma((2,)),
             dma((2,)),
+            dma,
+            dma((2 * outer,)),
+            dma,
+            dma((2 * outer,)),
             dma((2,)),
             dma((2 * outer + 1,)),
         ],

time: 28.5 us -> 28 us (0.982); the launches traced: 28.4 us -> 27.5 us
  Pallas kernels: 27.7 us -> 26.9 us
    pallas_call x1, Pallas kernels: 26.8 us -> 26 us  [shards(): pl.pallas_call(functools.partial(sweep_kernel, inner, outer, deep, nwid,...]
where the time goes in v3:
time: 28 us; the launch traced here: 27.5 us
  Pallas kernels  26.9 us (96%)
  between operations  0.64 us (2%)
    pallas_call x1, Pallas kernels, shards(): pl.pallas_call(functools.partial(sweep_kernel, inner, outer, deep, nwid,...  26 us
    pallas_call x1, Pallas kernels, shards(): pl.pallas_call(store_kernel, out_shape=(out, out), in_specs=[anywhere] *...  0.89 us

profile of v3, /device:TPU:1, one launch (start us, length us, event | category | flops | bytes accessed | tf_op | source)
XLA Modules:
  0.0 27.5 jit_solution(7818899712340359034)
XLA Ops:
  0.6 26.0 %sweep.1 = (f32[3,8,16,256]{3,2,1,0:T(8,128)S(1)}, f32[3,8,16,256]{3,2,1,0:T(8,128)S(1)}) custom-call(f32[3,8,16,256]{3,2,1,0:T(8,128)} %flow_hbm.1, f32[8,16,256]{2,1,0:T(8,128)} %cour_hbm.1, f32[3,16,256]{2,1,0:T(8,128)} %inflow_hbm.1, f32[8,16,16]{2,1,0:T(8,128)} %ops_hbm.1, s32[2]{0:T(128)} %metric_hbm.1), custom_call_target="tpu_custom_call" | custom-call | tf_op jit(solution)/shard_map/sweep/pallas_call | solution.py:510
  26.6 0.9 %finish.1 = (f32[3,8,16,256]{3,2,1,0:T(8,128)}, f32[3,8,16,256]{3,2,1,0:T(8,128)}) custom-call(f32[3,8,16,256]{3,2,1,0:T(8,128)S(1)} %get-tuple-element.4.new_in, f32[3,8,16,256]{3,2,1,0:T(8,128)S(1)} %get-tuple-element.5.tend_in), custom_call_target="tpu_custom_call" | custom-call | tf_op jit(solution)/shard_map/finish/pallas_call | solution.py:550

commit v4 on v3

--- a/solution.py
+++ b/solution.py
@@ -39,7 +39,9 @@
     wid = lax.axis_index("wid")
     mine = lax.rem(me, inner)
     block = lax.div(me, inner)
-    right, left = lax.rem(wid + 1, nwid), lax.rem(wid + nwid - 1, nwid)
+    right, left = jnp.minimum(wid + 1, nwid - 1), jnp.maximum(wid - 1, 0)
+    has_left, has_right = wid > 0, wid < nwid - 1
+    beside = jnp.where(has_left, 1, 0) + jnp.where(has_right, 1, 0)
 
     loads = [
         pltpu.make_async_copy(src, dst, in_sem.at[i])
@@ -62,8 +64,14 @@
     def greet(to, across):
         pl.semaphore_signal(barrier, inc=1, device_id=(to, across), device_id_type=MESH)
 
-    greet(me, left)
-    greet(me, right)
+    @pl.when(has_left)
+    def _():
+        greet(me, left)
+
+    @pl.when(has_right)
+    def _():
+        greet(me, right)
+
     seats = [seat(w) for w in range(owners)]
     for t in seats:
         @pl.when(me != t)
@@ -75,8 +83,26 @@
         for t in range(count):
             if t not in seats:
                 greet(t, wid)
+
+    @pl.when(jnp.logical_and(owner, has_left))
+    def _():
+        for t in range(count):
             greet(t, left)
+
+    @pl.when(jnp.logical_and(owner, has_right))
+    def _():
+        for t in range(count):
             greet(t, right)
+
+    @pl.when(jnp.logical_not(has_left))
+    def _():
+        halo_in[1] = jnp.zeros_like(halo_in[1])
+        edge_in[:per * count] = jnp.zeros((per * count, 1, LANE), jnp.float32)
+
+    @pl.when(jnp.logical_not(has_right))
+    def _():
+        halo_in[0] = jnp.zeros_like(halo_in[0])
+        edge_in[per * count:] = jnp.zeros((per * count, 1, LANE), jnp.float32)
 
     row = lax.broadcasted_iota(jnp.int32, (SUB, LANE), 0)
     lane = lax.broadcasted_iota(jnp.int32, (SUB, LANE), 1)
@@ -125,11 +151,11 @@
 
     @pl.when(owner)
     def _():
-        pl.semaphore_wait(barrier, 2 + count - 1 + 2 * owners)
+        pl.semaphore_wait(barrier, count - 1 + (1 + owners) * beside)
 
     @pl.when(jnp.logical_not(owner))
     def _():
-        pl.semaphore_wait(barrier, 2 + 3 * owners)
+        pl.semaphore_wait(barrier, owners + (1 + owners) * beside)
 
     halos = [
         pltpu.make_async_remote_copy(
@@ -142,10 +168,10 @@
         )
         for side, to in ((0, left), (1, right))
     ]
-    def far_first(act):
-        for j in sorted(range(outer), key=lambda j: -min(j, outer - j)):
+    def to_owners(act):
+        for j in range(outer):
             to = lax.rem(block + j, outer)
-            for r in range(deep):
+            for r in reversed(range(deep)):
                 act(j, to + outer * r, to * inner + (SHIFT + r) % inner)
 
     def edge_copy(side, across, w, device, p):
@@ -158,14 +184,34 @@
             device_id_type=MESH,
         )
 
+    def edge_span(parts, q):
+        span = edge_in.at[pl.ds(0, parts * per)]
+        return pltpu.make_async_remote_copy(
+            src_ref=span, dst_ref=span, send_sem=edge_send, recv_sem=edge_recv.at[q],
+            device_id=(me, wid), device_id_type=MESH,
+        )
+
     def give_edges(j, w, device):
         for p in range(per):
-            edge_copy(0, left, w, device, p).start()
-            edge_copy(1, right, w, device, p).start()
-
-    far_first(give_edges)
-    for halo in halos:
-        halo.start()
+            @pl.when(has_left)
+            def _():
+                edge_copy(0, left, w, device, p).start()
+
+            @pl.when(has_right)
+            def _():
+                edge_copy(1, right, w, device, p).start()
+
+    to_owners(give_edges)
+    def each_halo(sent, got):
+        for there, go, come in ((has_left, 0, 1), (has_right, 1, 0)):
+            @pl.when(there)
+            def _():
+                if sent:
+                    sent(halos[go])
+                if got:
+                    got(halos[come])
+
+    each_halo(lambda halo: halo.start(), None)
 
     loads[4].wait()
     loads[3].wait()
@@ -226,7 +272,7 @@
         else:
             pl.when(me != device)(give)
 
-    far_first(give_pulls)
+    to_owners(give_pulls)
 
     def edge_terms(at_start, at_end, pull):
         lanes = lax.broadcasted_iota(jnp.int32, pull.shape, 1)
@@ -339,14 +385,13 @@
         else:
             pl.when(me != device)(give)
 
-    far_first(give_map)
-
-    for halo in halos:
-        halo.wait_recv()
+    to_owners(give_map)
+
+    each_halo(None, lambda halo: halo.wait_recv())
     for h in range(nh):
         z = slice(h * SUB, (h + 1) * SUB)
-        fix_start = jnp.where(wid == 0, 0.0, halo_in[1, h])
-        fix_end = jnp.where(wid == nwid - 1, 0.0, halo_in[0, h])
+        fix_start = halo_in[1, h]
+        fix_end = halo_in[0, h]
         for l in {0, nl - 1}:
             y = slice(l * LANE, (l + 1) * LANE)
             for f in range(fields):
@@ -375,7 +420,7 @@
             span = pull_in.at[pl.ds(0, parts * per)]
             pltpu.make_async_remote_copy(
                 src_ref=span, dst_ref=span, send_sem=pull_send, recv_sem=pull_recv.at[q],
-                device_id=(me, right), device_id_type=MESH,
+                device_id=(me, wid), device_id_type=MESH,
             ).wait_recv()
 
         entries = list(starts)
@@ -401,16 +446,16 @@
                 pull_wait(half, q)
                 total(recv1, half, 0, q).wait_recv()
 
-            span = edge_in.at[pl.ds(0, 2 * half * per)]
-            pltpu.make_async_remote_copy(
-                src_ref=span, dst_ref=span, send_sem=edge_send, recv_sem=edge_recv.at[q],
-                device_id=(me, right), device_id_type=MESH,
-            ).wait_recv()
+            for sides in (1, 2):
+                @pl.when(beside == sides)
+                def _():
+                    edge_span(sides * half, q).wait_recv()
+
             for p in range(per):
                 at = p * count + q * half
                 terms = edge_terms(
-                    jnp.where(wid == 0, 0.0, edge_in[at:at + half, 0, :]),
-                    jnp.where(wid == nwid - 1, 0.0, edge_in[per * count + at:per * count + at + half, 0, :]),
+                    edge_in[at:at + half, 0, :],
+                    edge_in[per * count + at:per * count + at + half, 0, :],
                     pull_in[at:at + half, 0, :],
                 )
                 for f in range(fields):
@@ -451,19 +496,17 @@
                 for i in range(nx):
                     new_ref[f, i, z, y] += prod[i, z, y] * enter
 
-    for halo in halos:
-        halo.wait_send()
-    span = edge_in.at[pl.ds(0, 2 * owners * per)]
-    pltpu.make_async_remote_copy(
-        src_ref=span, dst_ref=span, send_sem=edge_send, recv_sem=edge_recv.at[0],
-        device_id=(me, right), device_id_type=MESH,
-    ).wait_send()
+    each_halo(lambda halo: halo.wait_send(), None)
+    for sides in (1, 2):
+        @pl.when(beside == sides)
+        def _():
+            edge_span(sides * owners, 0).wait_send()
 
     def pull_sent(parts):
         span = pull_in.at[pl.ds(0, parts * per)]
         pltpu.make_async_remote_copy(
             src_ref=span, dst_ref=span, send_sem=pull_send, recv_sem=pull_recv.at[0],
-            device_id=(me, right), device_id_type=MESH,
+            device_id=(me, wid), device_id_type=MESH,
         ).wait_send()
 
     @pl.when(owner)

time: 28 us -> 27.2 us (0.971)
  the two profiles are of different devices: /device:TPU:1 before, /device:TPU:31 now
where the time goes in v4:
time: 27.2 us; the launch traced here: 27.1 us
  Pallas kernels  26.5 us (97%)
  between operations  0.64 us (2%)
    pallas_call x1, Pallas kernels, shards(): pl.pallas_call(functools.partial(sweep_kernel, inner, outer, deep, nwid,...  25.6 us
    pallas_call x1, Pallas kernels, shards(): pl.pallas_call(store_kernel, out_shape=(out, out), in_specs=[anywhere] *...  0.89 us

profile of v4, /device:TPU:31, one launch (start us, length us, event | category | flops | bytes accessed | tf_op | source)
XLA Modules:
  0.0 27.1 jit_solution(3706291713563172442)
XLA Ops:
  0.6 25.6 %sweep.1 = (f32[3,8,16,256]{3,2,1,0:T(8,128)S(1)}, f32[3,8,16,256]{3,2,1,0:T(8,128)S(1)}) custom-call(f32[3,8,16,256]{3,2,1,0:T(8,128)} %flow_hbm.1, f32[8,16,256]{2,1,0:T(8,128)} %cour_hbm.1, f32[3,16,256]{2,1,0:T(8,128)} %inflow_hbm.1, f32[8,16,16]{2,1,0:T(8,128)} %ops_hbm.1, s32[2]{0:T(128)} %metric_hbm.1), custom_call_target="tpu_custom_call" | custom-call | tf_op jit(solution)/shard_map/sweep/pallas_call | solution.py:553
  26.2 0.9 %finish.1 = (f32[3,8,16,256]{3,2,1,0:T(8,128)}, f32[3,8,16,256]{3,2,1,0:T(8,128)}) custom-call(f32[3,8,16,256]{3,2,1,0:T(8,128)S(1)} %get-tuple-element.4.new_in, f32[3,8,16,256]{3,2,1,0:T(8,128)S(1)} %get-tuple-element.5.tend_in), custom_call_target="tpu_custom_call" | custom-call | tf_op jit(solution)/shard_map/finish/pallas_call | solution.py:593

commit v5 on v4

--- a/solution.py
+++ b/solution.py
@@ -24,16 +24,15 @@
     flow_hbm, cour_hbm, inflow_hbm, ops_hbm, metric_hbm,
     new_ref, tend_ref,
     flow, cour, infl, ops, metric, prod, keep, gain, halo_out, halo_in,
-    edge_out, edge_in, pull_out, pull_in, edge_tiles,
+    edge_out, edge_in, edge_tiles,
     send1, recv1, send3, recv3,
-    in_sem, halo_send, halo_recv, edge_send, edge_recv, pull_send, pull_recv, ex_send, ex_recv,
+    in_sem, halo_send, halo_recv, edge_send, edge_recv, ex_send, ex_recv,
 ):
     fields, nx, nz, ny = flow.shape
     nh, nl = nz // SUB, ny // LANE
     count = inner * outer
     owners = deep * outer
     per = nz // owners
-    chunk = per * SUB
     half = inner // 2
     me = lax.axis_index("len")
     wid = lax.axis_index("wid")
@@ -111,6 +110,8 @@
     sections = 2 * outer
     field_lanes = nx * 4
     states = fields * nl
+    full = states + 1 + nl
+    chunk = per * full
     back_rows = per * states
 
     ahead = lax.broadcasted_iota(jnp.int32, (ny, ny), 0) - lax.broadcasted_iota(jnp.int32, (ny, ny), 1)
@@ -250,29 +251,11 @@
             tiles[h] = jnp.where(slot == nx + i, turned, tiles[h])
     for h in range(nh):
         pulls.append(jnp.where(spot < 3, tiles[h], 0.0))
-        pull_out[h * SUB:(h + 1) * SUB, 0, :] = pulls[h]
-
-    def pull_copy(w, device, p):
-        return pltpu.make_async_remote_copy(
-            src_ref=pull_out.at[pl.ds(w * per + p, 1)],
-            dst_ref=pull_in.at[pl.ds(p * count + me, 1)],
-            send_sem=pull_send,
-            recv_sem=pull_recv.at[section],
-            device_id=(device, wid),
-            device_id_type=MESH,
-        )
-
-    def give_pulls(j, w, device):
-        def give():
-            for p in range(per):
-                pull_copy(w, device, p).start()
-
-        if j:
-            give()
-        else:
-            pl.when(me != device)(give)
-
-    to_owners(give_pulls)
+        send1[pl.ds(h * SUB * full + states, SUB, stride=full), 0, :] = pulls[h]
+        for l in range(nl):
+            send1[pl.ds(h * SUB * full + states + 1 + l, SUB, stride=full), 0, :] = prod[
+                nx - 1, h * SUB:(h + 1) * SUB, l * LANE:(l + 1) * LANE
+            ]
 
     def edge_terms(at_start, at_end, pull):
         lanes = lax.broadcasted_iota(jnp.int32, pull.shape, 1)
@@ -325,13 +308,12 @@
             new_ref[f, i] = cour[i] * (flow[f, i] + STEP * tend)
 
     def scatter(tile, v, h, l):
-        send1[pl.ds(h * SUB * SUB + v * nl + l, SUB, stride=SUB), :] = tile
+        send1[pl.ds(h * SUB * full + v * nl + l, SUB, stride=full), 0, :] = tile
 
     for h in range(nh):
         z = slice(h * SUB, (h + 1) * SUB)
         for l in range(nl):
             y = slice(l * LANE, (l + 1) * LANE)
-            scatter(prod[nx - 1, z, y], fields, h, l)
             for f in range(fields):
                 state = None
                 for i in range(nx):
@@ -350,35 +332,18 @@
             device_id_type=MESH,
         )
 
-    def rows_of(k):
-        return pl.ds(k * chunk if isinstance(k, int) else pl.multiple_of(k * chunk, SUB), chunk)
-
-    def part(ref, k):
-        return ref.at[rows_of(k), :]
-
-    def total(ref, parts, phase, slot):
-        span = ref.at[pl.ds(0, parts * chunk), :]
+    def part(ref, k, size):
+        return ref.at[pl.ds(k * size, size)]
+
+    def total(ref, parts, phase, slot, size):
+        span = ref.at[pl.ds(0, parts * size)]
         return remote(span, span, phase, slot, me)
 
-    def load_map(ref, at):
-        tile = ref[at:at + SUB, :]
-        decay = jnp.broadcast_to(tile[states:states + 1], (SUB, LANE))
-        for l in range(1, nl):
-            decay = jnp.where(row % nl == l, jnp.broadcast_to(tile[states + l:states + l + 1], (SUB, LANE)), decay)
-        return decay, tile
-
     back = sections
-
-    def back_part(ref, k):
-        return ref.at[pl.ds(k * back_rows, back_rows)]
-
-    def back_total(ref, parts):
-        span = ref.at[pl.ds(0, parts * back_rows)]
-        return remote(span, span, 1, back, me)
 
     def give_map(j, w, device):
         def give():
-            remote(part(send1, w), part(recv1, me), 0, section, device).start()
+            remote(part(send1, w, chunk), part(recv1, me, chunk), 0, section, device).start()
 
         if j:
             give()
@@ -412,23 +377,14 @@
 
     @pl.when(owner)
     def _():
-        recv1[rows_of(me), :] = send1[rows_of(rank), :]
-        for p in range(per):
-            pull_in[pl.ds(p * count + me, 1)] = pull_out[pl.ds(rank * per + p, 1)]
-
-        def pull_wait(parts, q):
-            span = pull_in.at[pl.ds(0, parts * per)]
-            pltpu.make_async_remote_copy(
-                src_ref=span, dst_ref=span, send_sem=pull_send, recv_sem=pull_recv.at[q],
-                device_id=(me, wid), device_id_type=MESH,
-            ).wait_recv()
-
-        entries = list(starts)
+        recv1[pl.ds(me * chunk, chunk)] = send1[pl.ds(rank * chunk, chunk)]
+        entries = [start[:states] for start in starts]
+        lines = lax.broadcasted_iota(jnp.int32, (states, LANE), 0)
 
         def send_back(q):
             for t in range(q * half, (q + 1) * half):
                 def give():
-                    remote(back_part(send3, t), back_part(recv3, rank), 1, back, t).start()
+                    remote(part(send3, t, back_rows), part(recv3, rank, back_rows), 1, back, t).start()
 
                 if t in seats:
                     pl.when(me != t)(give)
@@ -438,13 +394,11 @@
         for q in range(sections):
             @pl.when(section == q)
             def _():
-                pull_wait(half - 1, q)
-                total(recv1, half - 1, 0, q).wait_recv()
+                total(recv1, half - 1, 0, q, chunk).wait_recv()
 
             @pl.when(section != q)
             def _():
-                pull_wait(half, q)
-                total(recv1, half, 0, q).wait_recv()
+                total(recv1, half, 0, q, chunk).wait_recv()
 
             for sides in (1, 2):
                 @pl.when(beside == sides)
@@ -456,7 +410,7 @@
                 terms = edge_terms(
                     edge_in[at:at + half, 0, :],
                     edge_in[per * count + at:per * count + at + half, 0, :],
-                    pull_in[at:at + half, 0, :],
+                    recv1[pl.ds(q * half * chunk + p * full + states, half, stride=chunk), 0, :],
                 )
                 for f in range(fields):
                     for l in range(nl):
@@ -469,12 +423,14 @@
 
             for t in range(q * half, (q + 1) * half):
                 for p in range(per):
-                    at = t * chunk + p * SUB
-                    send3[t * back_rows + p * states:t * back_rows + (p + 1) * states, 0, :] = entries[p][:states]
-                    decay, state = load_map(recv1, at)
-                    edge = edge_tiles[(p * count + t) * SUB:(p * count + t + 1) * SUB, :]
-                    edge = jnp.where(row < states, edge, 0.0)
-                    entries[p] = decay * entries[p] + (state + edge)
+                    at = t * back_rows + p * states
+                    send3[at:at + states, 0, :] = entries[p]
+                    decay = jnp.zeros((states, LANE), jnp.float32)
+                    for l in range(nl):
+                        line = recv1[t * chunk + p * full + states + 1 + l]
+                        decay = jnp.where(lines % nl == l, jnp.broadcast_to(line, (states, LANE)), decay)
+                    edge = edge_tiles[(p * count + t) * SUB:(p * count + t) * SUB + states, :]
+                    entries[p] = decay * entries[p] + (recv1[t * chunk + p * full:t * chunk + p * full + states, 0, :] + edge)
             if q % 2 == 0:
                 send_back(q)
                 if q > 2:
@@ -482,11 +438,11 @@
         send_back(sections - 3)
         send_back(sections - 1)
         recv3[pl.ds(rank * back_rows, back_rows)] = send3[pl.ds(me * back_rows, back_rows)]
-        back_total(recv3, owners - 1).wait_recv()
+        total(recv3, owners - 1, 1, back, back_rows).wait_recv()
 
     @pl.when(jnp.logical_not(owner))
     def _():
-        back_total(recv3, owners).wait_recv()
+        total(recv3, owners, 1, back, back_rows).wait_recv()
 
     for f in range(fields):
         for h in range(nh):
@@ -502,23 +458,14 @@
         def _():
             edge_span(sides * owners, 0).wait_send()
 
-    def pull_sent(parts):
-        span = pull_in.at[pl.ds(0, parts * per)]
-        pltpu.make_async_remote_copy(
-            src_ref=span, dst_ref=span, send_sem=pull_send, recv_sem=pull_recv.at[0],
-            device_id=(me, wid), device_id_type=MESH,
-        ).wait_send()
-
     @pl.when(owner)
     def _():
-        pull_sent(owners - 1)
-        total(send1, owners - 1, 0, 0).wait_send()
-        back_total(send3, count - 1).wait_send()
+        total(send1, owners - 1, 0, 0, chunk).wait_send()
+        total(send3, count - 1, 1, back, back_rows).wait_send()
 
     @pl.when(jnp.logical_not(owner))
     def _():
-        pull_sent(owners)
-        total(send1, owners, 0, 0).wait_send()
+        total(send1, owners, 0, 0, chunk).wait_send()
 
 
 def store_kernel(new_in, tend_in, new_out, tend_out, sem):
@@ -538,7 +485,7 @@
     nwid = lax.axis_size("wid")
     outer = count // inner
     owners = deep * outer
-    chunk = nz // owners * SUB
+    full = (fields + 1) * (ny // LANE) + 1
     out = jax.ShapeDtypeStruct(flow_state.shape, jnp.float32)
     anywhere = pl.BlockSpec(memory_space=pl.ANY)
     nh = nz // SUB
@@ -568,18 +515,14 @@
             pltpu.VMEM((2, nh, SUB, LANE), f32),
             pltpu.VMEM((2 * nz, 1, LANE), f32),
             pltpu.VMEM((2 * heights, 1, LANE), f32),
-            pltpu.VMEM((nz, 1, LANE), f32),
-            pltpu.VMEM((heights, 1, LANE), f32),
             pltpu.VMEM((heights * SUB, LANE), f32),
-            pltpu.VMEM((owners * chunk, LANE), f32),
-            pltpu.VMEM((count * chunk, LANE), f32),
+            pltpu.VMEM((nz * full, 1, LANE), f32),
+            pltpu.VMEM((heights * full, 1, LANE), f32),
             pltpu.VMEM((heights * states, 1, LANE), f32),
             pltpu.VMEM((nz * states, 1, LANE), f32),
             dma((5,)),
             dma((2,)),
             dma((2,)),
-            dma,
-            dma((2 * outer,)),
             dma,
             dma((2 * outer,)),
             dma((2,)),

time: 27.2 us -> 27.1 us (level)
  no operation moved by 1% of the time
where the time goes in v5:
time: 27.1 us; the launch traced here: 27 us
  Pallas kernels  26.4 us (97%)
  between operations  0.64 us (2%)
    pallas_call x1, Pallas kernels, shards(): pl.pallas_call(functools.partial(sweep_kernel, inner, outer, deep, nwid,...  25.5 us
    pallas_call x1, Pallas kernels, shards(): pl.pallas_call(store_kernel, out_shape=(out, out), in_specs=[anywhere] *...  0.89 us

profile of v5, /device:TPU:31, one launch (start us, length us, event | category | flops | bytes accessed | tf_op | source)
XLA Modules:
  0.0 27.0 jit_solution(8639837210511432897)
XLA Ops:
  0.6 25.5 %sweep.1 = (f32[3,8,16,256]{3,2,1,0:T(8,128)S(1)}, f32[3,8,16,256]{3,2,1,0:T(8,128)S(1)}) custom-call(f32[3,8,16,256]{3,2,1,0:T(8,128)} %flow_hbm.1, f32[8,16,256]{2,1,0:T(8,128)} %cour_hbm.1, f32[3,16,256]{2,1,0:T(8,128)} %inflow_hbm.1, f32[8,16,16]{2,1,0:T(8,128)} %ops_hbm.1, s32[2]{0:T(128)} %metric_hbm.1), custom_call_target="tpu_custom_call" | custom-call | tf_op jit(solution)/shard_map/sweep/pallas_call | solution.py:500
  26.1 0.9 %finish.1 = (f32[3,8,16,256]{3,2,1,0:T(8,128)}, f32[3,8,16,256]{3,2,1,0:T(8,128)}) custom-call(f32[3,8,16,256]{3,2,1,0:T(8,128)S(1)} %get-tuple-element.4.new_in, f32[3,8,16,256]{3,2,1,0:T(8,128)S(1)} %get-tuple-element.5.tend_in), custom_call_target="tpu_custom_call" | custom-call | tf_op jit(solution)/shard_map/finish/pallas_call | solution.py:536
